TPU v7x, 128 devices: a whole 4x4x4 slice. The times are simulated.
128 devices in a mesh: cluster: 128 (over z, y, x, core).
Axes of the slice: x: 4, y: 4, z: 4, core: 2. Of those that a mesh axis runs over, the one named last changes fastest.
Arguments:
- charges: bfloat16 [16384, 16, 128], P('cluster'), may hold values from -6 to 6
- points: float32 [16384, 3, 128], P('cluster'), may hold values from 0 to 16384, as said below
- basis: bfloat16 [16384, 32, 128], P('cluster'), may hold values from -0.5 to 0.5
- near_list: int32 [16384, 3], P('cluster'), may hold values from -1 to 16383, as said below
- loc_coupling: bfloat16 [128, 248, 3, 1024], P('cluster'), may hold values from -0.625 to 0.625
- loc_transfer: bfloat16 [128, 248, 1024], P('cluster'), may hold values from -0.875 to 0.875
- loc_lists: int32 [128, 248, 3], P('cluster'), may hold values from -1 to 16383, as said below
- top_coupling: bfloat16 [1020, 3, 1024], replicated, may hold values from -0.625 to 0.625
- top_transfer: bfloat16 [1016, 1024], replicated, may hold values from -0.875 to 0.875
- top_lists: int32 [1020, 3], replicated, may hold values from -1 to 511, as said below
Outputs:
- potential: float32 [16384, 16, 128], P('cluster')
Inputs may be any that keep to these rules, and one draw needn't show every extreme that they name: `near_list`: slot entries of leaf i are distinct; each is -1 or a leaf j with |j - i| <= 1; i itself is always listed. `loc_lists`: each entry of node c (on its level of n nodes) is -1 or a node j of that level with 2 <= |j - c| <= 3 and |floor(j / 2) - floor(c / 2)| <= 1; entries of one node are distinct. `top_lists`: as for loc_lists, on the coarse levels. `points`: component 0 of a panel of leaf i lies in [i, i + 1), the other two in [0, 1).
All inputs are finite; a program needn't handle non-finite values.
Results may differ from a plain program's by a relative error of at most 0.0029.
Values sent between devices are 32-bit elements; how exact they have to be, the bound alone decides.
No kernel may reach another device: no remote copies, remote signals or barrier semaphores. Data moves between devices by JAX's collectives and lax.ppermute only.
A program may use at most 192 MiB of HBM per device.

v0:
```python
import jax
import jax.numpy as jnp
from jax import lax
from jax.experimental import pallas as pl
from jax.experimental.pallas import tpu as pltpu
from jax.sharding import PartitionSpec as P

AREA_WEIGHT = 0.0625
SOFTENING = 0.0025
SCALE = 1.0 / AREA_WEIGHT

NK = 16
RANK = 32
LANES = 128
LEVELS = 7
F32 = jnp.float32
BF16 = jnp.bfloat16

NODES = [LANES >> level for level in range(8)]
FOLD = [min(NK, 1 << level) for level in range(8)]
PLANES = [NK // fold for fold in FOLD]
ROWS = [planes * RANK for planes in PLANES]
START = [sum(ROWS[:level]) for level in range(9)]
TILE_ROW = [0, 0, 64, 96, 112, 120, 124, 126]
HALO_LANE = [0, 2, 6, 14, 30, 62, 94]
M_ROWS = START[LEVELS]
HEAD = 24
FRAME = 8 * (LANES + 2)


def log2(value):
    return value.bit_length() - 1


def iota(shape, dim):
    return lax.broadcasted_iota(jnp.int32, shape, dim)


def ones_where(cond):
    return jnp.where(cond, 1.0, 0.0).astype(BF16)


def dot(a, b):
    return jnp.dot(a, b, preferred_element_type=F32)


def dot_nt(a, b):
    return lax.dot_general(a, b, (((1,), (1,)), ((), ())), preferred_element_type=F32)


def dot_tn(a, b):
    return lax.dot_general(a, b, (((0,), (0,)), ((), ())), preferred_element_type=F32)


def split(x):
    high = x.astype(BF16)
    low = (x - high.astype(F32)).astype(BF16)
    return high, low


def dot_exact(x, selection):
    high, low = split(x)
    return dot(high, selection) + dot(low, selection)


def eye():
    return ones_where(iota((LANES, LANES), 0) == iota((LANES, LANES), 1))


def pair_target(level, index):
    nodes = NODES[level]
    lane = index & (LANES - 1)
    node = lane & (nodes - 1)
    high = lane >> log2(nodes)
    if level < 4:
        half = index >> 7
        return high * nodes + half * (nodes // 2) + (node >> 1)
    return jnp.where(lane < NK * nodes, high * (nodes // 2) + (node >> 1), -1)


def pair_matrix(level):
    depth = 2 * LANES if level < 4 else LANES
    return ones_where(pair_target(level, iota((depth, LANES), 0)) == iota((depth, LANES), 1))


def pair_matrix_t(level):
    width = 2 * LANES if level < 4 else LANES
    return ones_where(pair_target(level, iota((LANES, width), 1)) == iota((LANES, width), 0))


def spread_matrix(level):
    nodes = NODES[level]
    row, lane = iota((LANES, LANES), 0), iota((LANES, LANES), 1)
    return ones_where((row == TILE_ROW[level] + (lane & (nodes - 1))) & (lane < FOLD[level] * nodes))


def turn_order():
    row, lane = iota((2 * LANES, 2 * LANES), 0), iota((2 * LANES, 2 * LANES), 1)
    return ones_where(row == (lane & (RANK - 1)) * 8 + (lane >> 5))


def transpose_swapped(order, rows_of, out_ref):
    for pair in range(4):
        turned = dot_nt(order, jnp.concatenate([rows_of(2 * pair), rows_of(2 * pair + 1)], axis=1))
        for t in range(RANK):
            out_ref[t * RANK + 8 * pair : t * RANK + 8 * pair + 8, :] = turned[8 * t : 8 * t + 8, :]


def extra_rows(four_ref, two_ref, d):
    four = pltpu.roll(four_ref[...].astype(F32), (8 - 4 * (d & 1)) & 7, 0)
    two = pltpu.roll(two_ref[...].astype(F32), (12 - 2 * (d & 3)) & 7, 0)
    row = iota((8, 1024), 0)
    return jnp.where(row < 4, four, jnp.where(row < 6, two, 0.0))


def head_rows(ref):
    return lambda c: ref[0:LANES, c * LANES : (c + 1) * LANES]


def tail_rows(ref, extra):
    def rows_of(c):
        cut = slice(c * LANES, (c + 1) * LANES)
        return jnp.concatenate([ref[LANES:248, cut].astype(F32), extra[:, cut]], axis=0).astype(BF16)

    return rows_of


def transpose_matrices(identity, rows_of, out_ref, base=0):
    for chunk in range(8):
        turned = dot_nt(identity, rows_of(chunk))
        out_ref[base + chunk * LANES : base + (chunk + 1) * LANES, :] = turned.astype(out_ref.dtype)


def spread_matrices(level, turned_ref, out_ref, base=0):
    spread = spread_matrix(level)
    for chunk in range(8):
        rows = slice(base + chunk * LANES, base + (chunk + 1) * LANES)
        out_ref[rows, :] = dot(turned_ref[rows, :].astype(BF16), spread)


def contract(plane_count, row_of, tile_of, store, init=None):
    block = min(4, plane_count)

    def run(first):
        if init is None:
            totals = [jnp.zeros((RANK, LANES), F32) for _ in range(block)]
        else:
            totals = [init(first + p) for p in range(block)]
        for r in range(RANK):
            tile = tile_of(r)
            for p in range(block):
                totals[p] = totals[p] + row_of(first + p, r) * tile
        for p in range(block):
            store(first + p, totals[p])

    if plane_count == block:
        run(0)
    else:
        lax.fori_loop(0, plane_count // block, lambda b, c: (run(b * block), c)[1], 0)


def plane_rows(plane):
    if isinstance(plane, int):
        return slice(plane * RANK, (plane + 1) * RANK)
    return pl.ds(pl.multiple_of(plane * RANK, RANK), RANK)


def climb(level, m_ref, source_base, matrix_ref, x_ref):
    def row_of(plane, r):
        return m_ref[pl.ds(source_base + plane * RANK + r, 1), :]

    def tile_of(r):
        return matrix_ref[r * RANK : (r + 1) * RANK, :]

    def store(plane, value):
        x_ref[plane_rows(plane), :] = value

    contract(PLANES[level], row_of, tile_of, store)


def pair_sum(level, x_ref):
    if level < 4:
        half = ROWS[level] // 2
        x = jnp.concatenate([x_ref[0:half, :], x_ref[half : 2 * half, :]], axis=1)
    else:
        x = x_ref[0:RANK, :]
    return dot_exact(x, pair_matrix(level))


def up_kernel(
    par_ref, ch_ref, pt_ref, ba_ref, e_ref, four_ref, two_ref, m_ref, near_msg, far_msg, top_ref, y_ref, x_ref, t_ref, w_ref
):
    d = par_ref[0]
    odd = d & 1
    first_leaf = [pt_ref[:, 0, :], ch_ref[0].astype(F32)]
    last_leaf = [pt_ref[:, LANES - 1, :], ch_ref[LANES - 1].astype(F32)]
    near_msg[0:HEAD, :] = jnp.zeros((HEAD, LANES), F32)
    far_msg[0:HEAD, :] = jnp.zeros((HEAD, LANES), F32)
    for rows, first, last in zip((slice(0, 3), slice(8, 24)), first_leaf, last_leaf):
        near_msg[rows, :] = jnp.where(odd == 1, first, last)
        far_msg[rows, :] = jnp.where(odd == 1, last, first)

    def leaf(i, carry):
        y_ref[pl.ds(pl.multiple_of(i * NK, NK), NK), 0:RANK] = dot_nt(ch_ref[i], ba_ref[i])
        return carry

    lax.fori_loop(0, LANES, leaf, 0, unroll=8)
    identity = eye()
    transpose_matrices(identity, head_rows(e_ref), w_ref)
    transpose_matrices(identity, tail_rows(e_ref, extra_rows(four_ref, two_ref, d)), t_ref)
    for k in range(NK):
        m_ref[k * RANK : (k + 1) * RANK, :] = y_ref[pl.ds(k, LANES, stride=NK), :].T[0:RANK, :]
    for level in range(LEVELS):
        if level > 0:
            spread_matrices(level, t_ref, w_ref)
        climb(level, m_ref, START[level], w_ref, x_ref)
        if level < LEVELS - 1:
            m_ref[START[level + 1] : START[level + 2], :] = pair_sum(level, x_ref)
    row, lane = iota((LANES, LANES), 0), iota((LANES, LANES), 1)
    spread = ones_where(((row >> 1) == (lane & (NK - 1))) & (row < 2 * NK))
    device = dot_exact(x_ref[0:RANK, :], spread)
    sub, lane8 = iota((8, LANES), 0), iota((8, LANES), 1)
    for a in range(4):
        kept = jnp.where(sub == (lane8 >> 4), device[8 * a : 8 * a + 8, :], 0.0)
        top_ref[:, a * LANES : (a + 1) * LANES] = jnp.broadcast_to(jnp.sum(kept, axis=0, keepdims=True), (LANES, LANES))
    for level in reversed(range(LEVELS)):
        nodes = NODES[level]
        row, lane = iota((LANES, 2 * LANES), 0), iota((LANES, 2 * LANES), 1)
        first = odd ^ (lane >> 7)
        slot = (lane & (LANES - 1)) - HALO_LANE[level]
        node = (slot & 1) + jnp.where(first == 1, 0, nodes - 2)
        wanted = (slot >> 1) * nodes + node
        pick = ones_where((slot >= 0) & (slot < 2 * FOLD[level]) & (row == wanted))
        picked = dot_exact(m_ref[START[level] : START[level + 1], :], pick)
        if level == LEVELS - 1:
            near_msg[HEAD:, :] = jnp.zeros((ROWS[0], LANES), F32)
            far_msg[HEAD:, :] = jnp.zeros((ROWS[0], LANES), F32)
        near_msg[HEAD : HEAD + ROWS[level], :] += picked[:, 0:LANES]
        far_msg[HEAD : HEAD + ROWS[level], :] += picked[:, LANES : 2 * LANES]


def couple_kernel(
    par_ref, m_ref, near_ref, far_ref, list_ref, top_list, s_ref, four_ref, two_ref, out_ref, src_ref, t_ref, w_ref, rel_ref
):
    d = par_ref[0]
    odd = (d & 1) == 1
    place = iota((1, LANES), 1)
    rel_ref[...] = jnp.full((8, 2 * LANES), 64.0, F32)
    start = jnp.where(place < 64, 0, jnp.where(place < 96, 64, jnp.where(place < 112, 96, 112)))
    count = jnp.where(place < 64, 64, jnp.where(place < 96, 32, jnp.where(place < 112, 16, 8)))
    for s in range(3):
        fine = list_ref[s, :, 0:LANES]
        rel_ref[s : s + 1, 0:LANES] = jnp.where(fine >= 0, fine - (d * LANES + place), 64).astype(F32)
        rest = list_ref[s, :, LANES:248]
        own = (d * count + place - start)[:, 0:120]
        rel_ref[s : s + 1, LANES:248] = jnp.where(rest >= 0, rest - own, 64).astype(F32)
        row = rel_ref[s : s + 1, LANES : 2 * LANES]
        for lane_at, base, nodes in ((120, 4 * d, 4), (124, 512 + 2 * d, 2)):
            for t in range(nodes):
                entry = top_list[s, base + t]
                index = (4 * d if nodes == 4 else 2 * d) + t
                value = jnp.where(entry >= 0, entry - index, 64).astype(F32)
                row = jnp.where(place == lane_at + t, value, row)
        rel_ref[s : s + 1, LANES : 2 * LANES] = row
    identity = eye()
    row = iota((LANES, LANES), 0)
    lane = iota((1, LANES), 1)
    for level in range(LEVELS):
        nodes, rows = NODES[level], ROWS[level]
        tile = 0 if level == 0 else 1
        for s in range(3):
            if level == 0:
                transpose_matrices(identity, head_rows(s_ref.at[s]), w_ref, s * 1024)
                extra = extra_rows(four_ref.at[s], two_ref.at[s], d)
                transpose_matrices(identity, tail_rows(s_ref.at[s], extra), t_ref, s * 1024)
            else:
                spread_matrices(level, t_ref, w_ref, s * 1024)
        rel = rel_ref[:, tile * LANES : (tile + 1) * LANES]
        if level > 0:
            rel = dot(rel.astype(BF16), spread_matrix(level))
        rel = rel.astype(jnp.int32)
        moments = m_ref[START[level] : START[level + 1], :]
        near_part, far_part = near_ref[HEAD : HEAD + rows, :], far_ref[HEAD : HEAD + rows, :]
        left = split(jnp.where(odd, near_part, far_part))
        right = split(jnp.where(odd, far_part, near_part))
        own = split(moments)
        node = lane & (nodes - 1)
        high = lane >> log2(nodes)
        for s in range(3):
            shift = rel[s : s + 1, :]
            target = node + shift
            usable = (shift >= -3) & (shift <= 3)
            inside = usable & (target >= 0) & (target < nodes)
            at_own = jnp.where(inside, high * nodes + target, -1)
            at_left = jnp.where(usable & (target < 0), HALO_LANE[level] + 2 * high + target + 2, -1)
            at_right = jnp.where(usable & (target >= nodes), HALO_LANE[level] + 2 * high + target - nodes, -1)
            total = None
            for part, at in ((own, at_own), (left, at_left), (right, at_right)):
                pick = ones_where(row == at)
                piece = dot(part[0], pick) + dot(part[1], pick)
                total = piece if total is None else total + piece
            src_ref[s * 512 : s * 512 + rows, :] = total

        base = START[level]

        def init(plane):
            return jnp.zeros((RANK, LANES), F32)

        def store(plane, value):
            out_ref[pl.ds(pl.multiple_of(base + plane * RANK, RANK), RANK), :] = value

        block = min(4, PLANES[level])

        def run(first):
            def slot(s, totals):
                totals = list(totals)
                for r in range(RANK):
                    tile_rows = w_ref[pl.ds(pl.multiple_of(s * 1024 + r * RANK, RANK), RANK), :]
                    for p in range(block):
                        at = s * 512 + (first + p) * RANK + r
                        totals[p] = totals[p] + src_ref[pl.ds(at, 1), :] * tile_rows
                return tuple(totals)

            totals = lax.fori_loop(0, 3, slot, tuple(init(p) for p in range(block)))
            for p in range(block):
                store(first + p, totals[p])

        if PLANES[level] == block:
            run(0)
        else:
            lax.fori_loop(0, PLANES[level] // block, lambda b, c: (run(b * block), c)[1], 0)


def top_kernel(par_ref, list_ref, g_ref, e_ref, s_ref, out_ref, m0_ref, m_ref, x_ref, t_ref, w_ref, src_ref, so_t, eo_t):
    d = par_ref[0]
    identity = eye()
    for a in range(4):
        m0_ref[a * LANES : (a + 1) * LANES, :] = g_ref[:, a * LANES : (a + 1) * LANES].T
    for k in range(NK):
        m_ref[k * RANK : (k + 1) * RANK, :] = m0_ref[pl.ds(k, RANK, stride=NK), :]
    transpose_matrices(identity, lambda c: e_ref[0:LANES, c * LANES : (c + 1) * LANES], w_ref)
    known = iota((LANES, LANES), 0) < 120

    def last_rows(c):
        block = e_ref[LANES : 2 * LANES, c * LANES : (c + 1) * LANES].astype(F32)
        return jnp.where(known, block, 0.0).astype(BF16)

    transpose_matrices(identity, last_rows, t_ref)
    row, lane = iota((LANES, 2 * LANES), 0), iota((LANES, 2 * LANES), 1)
    level_of = row >> 4
    own_lane = jnp.where(level_of == 5, 248 + (d >> 5), -1)
    for level in range(5):
        own_lane = jnp.where(level_of == level, 256 - (256 >> level) + (d >> level), own_lane)
    own_rows = ones_where(lane == own_lane)
    filled = iota((2 * LANES, LANES), 0)

    def own_of(ref, rows):
        def rows_of(c):
            block = ref[:, c * LANES : (c + 1) * LANES].astype(F32)
            return dot(own_rows, jnp.where(filled < rows, block, 0.0).astype(BF16)).astype(BF16)

        return rows_of

    for s in range(3):
        transpose_matrices(identity, own_of(s_ref.at[s], 252), so_t, s * 1024)
    transpose_swapped(turn_order(), own_of(e_ref, 248), eo_t)
    for level in range(5):
        if level > 0:
            spread_matrices(level, t_ref, w_ref)
        climb(level, m_ref, START[level], w_ref, x_ref)
        m_ref[START[level + 1] : START[level + 2], :] = pair_sum(level, x_ref)
    row, lane = iota((LANES, LANES), 0), iota((LANES, LANES), 1)
    lane_r = iota((RANK, LANES), 1)
    sources = [jnp.zeros((RANK, LANES), F32) for _ in range(3)]
    for level in range(6):
        planes = PLANES[level]
        high = (lane & (NK - 1)) >> log2(planes)
        delta = row - high * NODES[level]
        here = (lane >> 4) == level
        entries = [list_ref[s, 1024 - (256 >> level) + (d >> level)] for s in range(3)]
        picks = [ones_where(here & (delta == jnp.where(e >= 0, e, -100000))) for e in entries]
        found = dot_exact(m_ref[START[level] : START[level + 1], :], jnp.concatenate(picks, axis=1))
        for plane in range(planes):
            mine = (lane_r & (planes - 1)) == plane
            for s in range(3):
                part = found[plane * RANK : (plane + 1) * RANK, s * LANES : (s + 1) * LANES]
                sources[s] = sources[s] + jnp.where(mine, part, 0.0)
    coupled = jnp.zeros((RANK, LANES), F32)
    for s in range(3):
        src_ref[s * RANK : (s + 1) * RANK, :] = sources[s]
    for s in range(3):
        for r in range(RANK):
            at = s * 1024 + r * RANK
            coupled = coupled + src_ref[s * RANK + r : s * RANK + r + 1, :] * so_t[at : at + RANK, :]
    local = coupled
    for level in reversed(range(5)):
        src_ref[0:RANK, :] = pltpu.roll(local, LANES - NK, 1)
        local = coupled
        for t in range(RANK):
            local = local + src_ref[t : t + 1, :] * eo_t[t * RANK : (t + 1) * RANK, :]
    out_ref[...] = local


def down_kernel(
    par_ref, top_ref, c_ref, e_ref, four_ref, two_ref, ba_ref, near_ref, out_ref, l_ref, p_ref, z_ref, t_ref, w_ref
):
    order = turn_order()
    transpose_swapped(order, tail_rows(e_ref, extra_rows(four_ref, two_ref, par_ref[0])), t_ref)
    l_ref[0:RANK, :] = top_ref[...]
    for level in reversed(range(LEVELS)):
        if level > 0:
            spread_matrices(level, t_ref, w_ref)
        else:
            transpose_swapped(order, head_rows(e_ref), w_ref)
        given = dot_exact(l_ref[0 : ROWS[level + 1], :], pair_matrix_t(level))
        if level < 4:
            half = ROWS[level + 1]
            p_ref[0:half, :] = given[:, 0:LANES]
            p_ref[half : 2 * half, :] = given[:, LANES : 2 * LANES]
        else:
            p_ref[0:RANK, :] = given

        def row_of(plane, t):
            return p_ref[pl.ds(plane * RANK + t, 1), :]

        def tile_of(t):
            return w_ref[t * RANK : (t + 1) * RANK, :]

        def init(plane):
            return c_ref[pl.ds(START[level] + plane * RANK, RANK), :]

        def store(plane, value):
            l_ref[plane_rows(plane), :] = value

        contract(PLANES[level], row_of, tile_of, store, init)
    for k in range(NK):
        z_ref[pl.ds(k, LANES, stride=NK), 0:RANK] = l_ref[k * RANK : (k + 1) * RANK, :].T

    def leaf(i, carry):
        local = z_ref[pl.ds(pl.multiple_of(i * NK, NK), NK), 0:RANK].astype(BF16)
        out_ref[i] = near_ref[i] + dot(local, ba_ref[i])
        return carry

    lax.fori_loop(0, LANES, leaf, 0, unroll=8)


def three(x):
    first = x.astype(BF16).astype(F32)
    rest = x - first
    second = rest.astype(BF16).astype(F32)
    return first, second, (rest - second).astype(BF16).astype(F32)


def near_kernel(par_ref, list_ref, pt_ref, ch_ref, near_msg, far_msg, out_ref, fa_ref, fs_ref, fn_ref, k_ref):
    d = par_ref[0]
    odd = (d & 1) == 1
    base = d * LANES
    left = jnp.where(odd, near_msg[...], far_msg[...])
    right = jnp.where(odd, far_msg[...], near_msg[...])
    soft = jnp.float32(SOFTENING) * (SCALE * SCALE)
    row8 = iota((FRAME, LANES), 0) & 7
    fa_ref[...] = jnp.where(row8 == 4, 1.0, 0.0)
    fs_ref[...] = jnp.where(row8 == 3, 1.0, 0.0)
    fn_ref[...] = jnp.where(row8 == 3, 1.0, 0.0)

    def features(values, first_leaf, put):
        x = ((values[0] - first_leaf.astype(F32)) - 0.5) * SCALE
        y, z = (values[1] - 0.5) * SCALE, (values[2] - 0.5) * SCALE
        moved = x + SCALE
        flat = y * y + z * z
        for j, value in enumerate((x, y, z, x * x + flat)):
            put(fa_ref, j, value)
        for ref, along in ((fs_ref, x), (fn_ref, moved)):
            for j, value in ((0, -2.0 * along), (1, -2.0 * y), (2, -2.0 * z), (4, along * along + flat + soft)):
                put(ref, j, value)

    def put_own(ref, j, value):
        ref[pl.ds(8 + j, LANES, stride=8), :] = value

    def put_left(ref, j, value):
        ref[j : j + 1, :] = value

    def put_right(ref, j, value):
        at = (LANES + 1) * 8 + j
        ref[at : at + 1, :] = value

    features([pt_ref[0], pt_ref[1], pt_ref[2]], iota((LANES, LANES), 0) + base, put_own)
    one_leaf = iota((1, LANES), 0) + base
    features([left[c : c + 1, :] for c in range(3)], one_leaf - 1, put_left)
    features([right[c : c + 1, :] for c in range(3)], one_leaf + LANES, put_right)

    def lists(i, offset):
        wanted = base + i + offset
        hit = (list_ref[0, i] == wanted) | (list_ref[1, i] == wanted) | (list_ref[2, i] == wanted)
        return jnp.where(hit, 1.0, 0.0).astype(F32)

    def pieces(ref, w):
        return three(ref[pl.ds(pl.multiple_of(w * 8, 8), 8), :])

    def source_of(w):
        a, b, c = pieces(fa_ref, w)
        return jnp.concatenate([a, a, b, b, a, c], axis=0).astype(BF16)

    def target_of(ref, w):
        a, b, c = pieces(ref, w)
        return jnp.concatenate([a, b, a, b, c, a], axis=0).astype(BF16)

    def kernel_of(source, target):
        return lax.rsqrt(dot_tn(source, target)).astype(BF16)

    first = dot(left[8:24, :].astype(BF16), kernel_of(source_of(0), target_of(fn_ref, 1)))

    def fill(i, carry):
        both = jnp.concatenate([target_of(fs_ref, i + 1), target_of(fn_ref, i + 2)], axis=1)
        k_ref[i] = kernel_of(source_of(i + 1), both)
        return carry

    lax.fori_loop(0, LANES, fill, 0, unroll=16)

    def step(i, carry, own, after):
        spread = dot(own, k_ref[i])
        back = dot_nt(after, k_ref[i, :, LANES : 2 * LANES])
        out_ref[i] = carry + spread[:, 0:LANES] + lists(i, 1) * back
        return spread[:, LANES : 2 * LANES]

    def body(i, carry):
        onward = step(i, carry, ch_ref[i], ch_ref[i + 1])
        return lists(i + 1, -1) * onward

    carry = lax.fori_loop(0, LANES - 1, body, lists(0, -1) * first, unroll=16)
    step(LANES - 1, carry, ch_ref[LANES - 1], right[8:24, :].astype(BF16))


VMEM = pl.BlockSpec(memory_space=pltpu.VMEM)
SMEM = pl.BlockSpec(memory_space=pltpu.SMEM)


def scratch(*shape, dtype=F32):
    return pltpu.VMEM(shape, dtype)


def shape(*dims):
    return jax.ShapeDtypeStruct(dims, F32)


def whole(*dims):
    return pl.BlockSpec(dims, lambda i, par: (0,) * len(dims))


NEAR_SCRATCH = [scratch(FRAME, LANES)] * 3 + [scratch(LANES, LANES, 2 * LANES, dtype=BF16)]
FOUR = pl.BlockSpec((8, 1024), lambda i, par: (par[0] >> 1, 0))
TWO = pl.BlockSpec((8, 1024), lambda i, par: (64 + (par[0] >> 2), 0))
FOUR_C = pl.BlockSpec((3, 8, 1024), lambda i, par: (0, par[0] >> 1, 0))
TWO_C = pl.BlockSpec((3, 8, 1024), lambda i, par: (0, 64 + (par[0] >> 2), 0))
LEAF_SPEC = pl.BlockSpec((HEAD, LANES), lambda i, par: (0, 0))


def call(kernel, name, in_specs, out_specs, out_shape, scratch_shapes):
    return pl.pallas_call(
        kernel,
        name=name,
        grid_spec=pltpu.PrefetchScalarGridSpec(
            num_scalar_prefetch=1,
            grid=(1,),
            in_specs=in_specs,
            out_specs=out_specs,
            scratch_shapes=scratch_shapes,
        ),
        out_shape=out_shape,
    )


def on_device(
    charges, points, basis, near_list, loc_coupling, loc_transfer, loc_lists, top_coupling, top_transfer, top_lists
):
    devices = lax.axis_size("cluster")
    d = lax.axis_index("cluster")
    mates = [(i, i ^ 1) for i in range(devices)]
    others = [(i, ((i + 1) ^ 1) - 1) for i in range(devices) if 0 <= ((i + 1) ^ 1) - 1 < devices]
    par = d.astype(jnp.int32).reshape(1)
    points_t = jnp.transpose(points, (1, 0, 2))
    transfer = loc_transfer[0]
    coupling = jnp.transpose(loc_coupling[0], (1, 0, 2))
    top_c = jnp.transpose(top_coupling, (1, 0, 2))
    top_l = jnp.transpose(top_lists)
    message = HEAD + ROWS[0]
    moments, msg_near, msg_far, device_moment = call(
        up_kernel,
        "up",
        [whole(LANES, NK, LANES), whole(3, LANES, LANES), whole(LANES, RANK, LANES), whole(248, 1024), FOUR, TWO],
        [whole(M_ROWS, LANES), whole(message, LANES), whole(message, LANES), whole(LANES, 512)],
        [shape(M_ROWS, LANES), shape(message, LANES), shape(message, LANES), shape(LANES, 512)],
        [scratch(2048, LANES), scratch(512, LANES), scratch(1024, LANES, dtype=BF16), scratch(1024, LANES)],
    )(par, charges, points_t, basis, transfer, top_transfer, top_transfer)

    halo_near = lax.ppermute(msg_near, "cluster", mates)
    halo_far = lax.ppermute(msg_far, "cluster", others)
    gathered = lax.all_to_all(device_moment, "cluster", 0, 0, tiled=True)

    near = call(
        near_kernel,
        "near",
        [SMEM, whole(3, LANES, LANES), whole(LANES, NK, LANES), LEAF_SPEC, LEAF_SPEC],
        whole(LANES, NK, LANES),
        shape(LANES, NK, LANES),
        NEAR_SCRATCH,
    )(par, near_list.T, points_t, charges, halo_near, halo_far)

    coupled = call(
        couple_kernel,
        "couple",
        [
            whole(M_ROWS, LANES),
            whole(message, LANES),
            whole(message, LANES),
            whole(3, 1, 248),
            SMEM,
            whole(3, 248, 1024),
            FOUR_C,
            TWO_C,
        ],
        whole(M_ROWS, LANES),
        shape(M_ROWS, LANES),
        [scratch(1536, LANES), scratch(3072, LANES, dtype=BF16), scratch(3072, LANES), scratch(8, 2 * LANES)],
    )(par, moments, halo_near, halo_far, jnp.transpose(loc_lists, (2, 0, 1)), top_l, coupling, top_c, top_c)

    top_local = call(
        top_kernel,
        "top",
        [
            SMEM,
            whole(LANES, 512),
            pl.BlockSpec((256, 1024), lambda i, par: (3, 0)),
            pl.BlockSpec((3, 256, 1024), lambda i, par: (0, 3, 0)),
        ],
        whole(RANK, LANES),
        shape(RANK, LANES),
        [
            scratch(512, LANES),
            scratch(START[6], LANES),
            scratch(512, LANES),
            scratch(1024, LANES, dtype=BF16),
            scratch(1024, LANES),
            scratch(96, LANES),
            scratch(3072, LANES),
            scratch(1024, LANES),
        ],
    )(par, top_l, gathered, top_transfer, top_c)

    return call(
        down_kernel,
        "down",
        [
            whole(RANK, LANES),
            whole(M_ROWS, LANES),
            whole(248, 1024),
            FOUR,
            TWO,
            whole(LANES, RANK, LANES),
            whole(LANES, NK, LANES),
        ],
        whole(LANES, NK, LANES),
        shape(LANES, NK, LANES),
        [
            scratch(512, LANES),
            scratch(512, LANES),
            scratch(2048, LANES),
            scratch(1024, LANES),
            scratch(1024, LANES),
        ],
    )(par, top_local, coupled, transfer, top_transfer, top_transfer, basis, near)


def solution(mesh):
    placed = (
        P("cluster", None, None),
        P("cluster", None, None),
        P("cluster", None, None),
        P("cluster", None),
        P("cluster", None, None, None),
        P("cluster", None, None),
        P("cluster", None, None),
        P(),
        P(),
        P(),
    )
    return jax.shard_map(
        on_device, mesh=mesh, in_specs=placed, out_specs=P("cluster", None, None), check_vma=False
    )
```

profile of v0, /device:TPU:1, one launch (start us, length us, event | category | flops | bytes accessed | tf_op | source)
XLA Modules:
  0.0 77.9 jit_solution(9826842129264849262)
XLA Ops:
  0.0 8.5 %up.1 = (f32[1056,128]{1,0:T(8,128)}, f32[536,128]{1,0:T(8,128)}, f32[536,128]{1,0:T(8,128)}, f32[128,512]{1,0:T(8,128)}) custom-call(s32[1]{0:T(128)} %bitcast.par_ref, bf16[128,16,128]{2,1,0:T(8,128)(2,1)} %ch_ref.3, f32[3,128,128]{2,1,0:T(8,128)} %bitcast.21, bf16[128,32,128]{2,1,0:T(8,128)(2,1)} %ba_ref.3, bf16[248,1024]{1,0:T(8,128)(2,1)} %bitcast.17, ...), custom_call_target="tpu_custom_call" | custom-call | tf_op jit(solution)/shard_map/up/pallas_call | solution.py:587
  8.5 1.4 %collective-permute-start = (f32[536,128]{1,0:T(8,128)}, f32[536,128]{1,0:T(8,128)S(1)}, u32[]{:S(2)}, u32[]{:S(2)}) collective-permute-start(f32[536,128]{1,0:T(8,128)} %get-tuple-element.11), channel_id=1, source_target_pairs={{0,1},{1,0},{2,3},{3,2},{4,5},{5,4},{6,7},{7,6},{8,9},{9,8},{10,11... | collective-permute-start | bytes 823304 | tf_op jit(solution)/shard_map/ppermute | solution.py:596
  9.9 3.1 %collective-permute-start.1 = (f32[536,128]{1,0:T(8,128)}, f32[536,128]{1,0:T(8,128)S(1)}, u32[]{:S(2)}, u32[]{:S(2)}) collective-permute-start(f32[536,128]{1,0:T(8,128)} %get-tuple-element.12), channel_id=1, source_target_pairs={{1,2},{2,1},{3,4},{4,3},{5,6},{6,5},{7,8},{8,7},{9,10},{10,9},{11,... | collective-permute-start | bytes 823304 | tf_op jit(solution)/shard_map/ppermute | solution.py:597
  13.0 1.2 %copy.11 = f32[128,1,512]{2,1,0:T(1,128)S(1)} copy(f32[128,1,512]{2,0,1:T(8,128)} %bitcast.23) | data formatting | bytes 524288 | tf_op jit(solution)/shard_map/all_to_all | solution.py:598
  14.3 20.7 %all_to_all.11 = f32[128,1,512]{2,1,0:T(1,128)S(1)} all-to-all(f32[128,1,512]{2,1,0:T(1,128)S(1)} %copy.11), channel_id=1, replica_groups=mesh['cluster'=128] {'cluster'}, dimensions={0} | all-to-all | bytes 524288 | tf_op jit(solution)/shard_map/all_to_all | solution.py:598
  35.0 0.7 copy.14
  35.7 7.6 %top.1.top_ref = f32[32,128]{1,0:T(8,128)} custom-call(s32[1]{0:T(128)} %bitcast.par_ref, s32[3,1020]{1,0:T(4,128)} %bitcast.24, f32[128,512]{1,0:T(8,128)} %bitcast.20, bf16[1016,1024]{1,0:T(8,128)(2,1)} %two_ref.3, bf16[3,1020,1024]{2,1,0:T(8,128)(2,1)} %bitcast.14), custom_call_target="tpu_custom_call" | custom-call | tf_op jit(solution)/shard_map/top/pallas_call | solution.py:627
  43.3 0.0 collective-permute-done.near_ref.near_msg
  43.3 0.0 copy-start
  43.3 0.0 collective-permute-done.1.far_ref.far_msg
  43.3 0.0 copy-start.1
  43.3 0.7 copy-done
  44.0 0.1 copy-done.1
  44.1 12.9 %near.1.near_ref = f32[128,16,128]{2,1,0:T(8,128)} custom-call(s32[1]{0:T(128)} %bitcast.par_ref, s32[3,128]{1,0:T(4,128)} %bitcast.27, f32[3,128,128]{2,1,0:T(8,128)} %bitcast.22, bf16[128,16,128]{2,1,0:T(8,128)(2,1)} %ch_ref.3, f32[536,128]{1,0:T(8,128)} %copy-done, f32[536,128]{1,0:T(8,128)} %copy-done.1), custom_call_target="tpu_custom_call" | custom-call | tf_op jit(solution)/shard_map/near/pallas_call | solution.py:600
  57.0 12.3 %couple.1.c_ref = f32[1056,128]{1,0:T(8,128)} custom-call(s32[1]{0:T(128)} %bitcast.par_ref, f32[1056,128]{1,0:T(8,128)} %get-tuple-element.10.m_ref, f32[536,128]{1,0:T(8,128)} %copy-done, f32[536,128]{1,0:T(8,128)} %copy-done.1, s32[3,1,248]{2,1,0:T(1,128)} %bitcast.26, s32[3,1020]{1,0:T(4,128)} %bitcast.25, bf16[3,248,1024]{2,1,0:T(8,128)(2,1)} %bitcast.19, ...), custom_call_target="tpu_custom_call" | custom-call | tf_op jit(solution)/shard_map/couple/pallas_call | solution.py:609
  69.3 8.6 %down.1 = f32[128,16,128]{2,1,0:T(8,128)} custom-call(s32[1]{0:T(128)} %bitcast.par_ref, f32[32,128]{1,0:T(8,128)} %top.1.top_ref, f32[1056,128]{1,0:T(8,128)} %couple.1.c_ref, bf16[248,1024]{1,0:T(8,128)(2,1)} %bitcast.18, bf16[1016,1024]{1,0:T(8,128)(2,1)} %two_ref.3, bf16[1016,1024]{1,0:T(8,128)(2,1)} %two_ref.3, bf16[128,32,128]{2,1,0:T(8,128)(2,1)} %ba_ref.3, ...), custom_call_target="tpu_custom_call" | custom-call | tf_op jit(solution)/shard_map/down/pallas_call | solution.py:650
Async XLA Ops:
  8.5 34.8 %collective-permute-start = (f32[536,128]{1,0:T(8,128)}, f32[536,128]{1,0:T(8,128)S(1)}, u32[]{:S(2)}, u32[]{:S(2)}) collective-permute-start(f32[536,128]{1,0:T(8,128)} %get-tuple-element.11), channel_id=1, source_target_pairs={{0,1},{1,0},{2,3},{3,2},{4,5},{5,4},{6,7},{7,6},{8,9},{9,8},{10,11... | collective-permute-start | bytes 823304 | tf_op jit(solution)/shard_map/ppermute | solution.py:596
  9.9 33.4 %collective-permute-start.1 = (f32[536,128]{1,0:T(8,128)}, f32[536,128]{1,0:T(8,128)S(1)}, u32[]{:S(2)}, u32[]{:S(2)}) collective-permute-start(f32[536,128]{1,0:T(8,128)} %get-tuple-element.12), channel_id=1, source_target_pairs={{1,2},{2,1},{3,4},{4,3},{5,6},{6,5},{7,8},{8,7},{9,10},{10,9},{11,... | collective-permute-start | bytes 823304 | tf_op jit(solution)/shard_map/ppermute | solution.py:597
  43.3 0.7 copy-start
  43.3 0.8 %copy-start.1 = (f32[536,128]{1,0:T(8,128)}, f32[536,128]{1,0:T(8,128)S(1)}, u32[]{:S(2)}) copy-start(f32[536,128]{1,0:T(8,128)S(1)} %collective-permute-done.1.far_ref.far_msg) | copy-start | bytes 823300
where the time goes:
time: 78.2 us; the launch traced here: 77.9 us
  Pallas kernels  50 us (64%)
  blocking collectives  20.7 us (26%)
  starting transfers between devices  4.49 us (6%)
  local copies, waits for them, and re-layouts  2.73 us (3%)
    all_to_all x1, blocking collectives, on_device(): gathered = lax.all_to_all(device_moment, 'cluster', 0, 0, tiled=True)  20.7 us
    pallas_call x1, Pallas kernels, on_device(): call(near_kernel, 'near', [SMEM, whole(3, LANES, LANES), whole(LANES, NK,...  12.9 us
    pallas_call x1, Pallas kernels, on_device(): call(couple_kernel, 'couple', [whole(M_ROWS, LANES), whole(message, LANES...  12.3 us
    pallas_call x1, Pallas kernels, on_device(): call(down_kernel, 'down', [whole(RANK, LANES), whole(M_ROWS, LANES), whol...  8.62 us
    pallas_call x1, Pallas kernels, on_device(): call(up_kernel, 'up', [whole(LANES, NK, LANES), whole(3, LANES, LANES), w...  8.53 us
    pallas_call x1, Pallas kernels, on_device(): call(top_kernel, 'top', [SMEM, whole(LANES, 512), pl.BlockSpec((256, 1024...  7.65 us
    ppermute x1, starting transfers between devices, on_device(): halo_far = lax.ppermute(msg_far, 'cluster', others)  3.11 us
  transfers between devices with their start and end apart: 2, of which 0 were waited for; matrix products, arithmetic and copies ran while one was open for 2% of the time, Pallas kernels for 10%

commit v1 on v0

--- a/solution.py
+++ b/solution.py
@@ -1,9 +1,12 @@
+import functools
+
 import jax
 import jax.numpy as jnp
 from jax import lax
 from jax.experimental import pallas as pl
 from jax.experimental.pallas import tpu as pltpu
 from jax.sharding import PartitionSpec as P
+
 
 AREA_WEIGHT = 0.0625
 SOFTENING = 0.0025
@@ -25,7 +28,10 @@
 HALO_LANE = [0, 2, 6, 14, 30, 62, 94]
 M_ROWS = START[LEVELS]
 HEAD = 24
-FRAME = 8 * (LANES + 2)
+PART = 32
+PARTS = LANES // PART
+AHEAD = 8
+FRAME = 8 * (PART + 2)
 
 
 def log2(value):
@@ -222,7 +228,7 @@
     sub, lane8 = iota((8, LANES), 0), iota((8, LANES), 1)
     for a in range(4):
         kept = jnp.where(sub == (lane8 >> 4), device[8 * a : 8 * a + 8, :], 0.0)
-        top_ref[:, a * LANES : (a + 1) * LANES] = jnp.broadcast_to(jnp.sum(kept, axis=0, keepdims=True), (LANES, LANES))
+        top_ref[:, a * LANES : (a + 1) * LANES] = jnp.sum(kept, axis=0, keepdims=True)
     for level in reversed(range(LEVELS)):
         nodes = NODES[level]
         row, lane = iota((LANES, 2 * LANES), 0), iota((LANES, 2 * LANES), 1)
@@ -240,6 +246,7 @@
 
 
 def couple_kernel(
+    levels,
     par_ref, m_ref, near_ref, far_ref, list_ref, top_list, s_ref, four_ref, two_ref, out_ref, src_ref, t_ref, w_ref, rel_ref
 ):
     d = par_ref[0]
@@ -265,14 +272,17 @@
     identity = eye()
     row = iota((LANES, LANES), 0)
     lane = iota((1, LANES), 1)
-    for level in range(LEVELS):
+    shift_rows = START[levels[0]]
+    if levels[0] > 0:
+        for s in range(3):
+            extra = extra_rows(four_ref.at[s], two_ref.at[s], d)
+            transpose_matrices(identity, tail_rows(s_ref.at[s], extra), t_ref, s * 1024)
+    for level in levels:
         nodes, rows = NODES[level], ROWS[level]
         tile = 0 if level == 0 else 1
         for s in range(3):
             if level == 0:
                 transpose_matrices(identity, head_rows(s_ref.at[s]), w_ref, s * 1024)
-                extra = extra_rows(four_ref.at[s], two_ref.at[s], d)
-                transpose_matrices(identity, tail_rows(s_ref.at[s], extra), t_ref, s * 1024)
             else:
                 spread_matrices(level, t_ref, w_ref, s * 1024)
         rel = rel_ref[:, tile * LANES : (tile + 1) * LANES]
@@ -301,9 +311,9 @@
                 total = piece if total is None else total + piece
             src_ref[s * 512 : s * 512 + rows, :] = total
 
-        base = START[level]
-
-        def init(plane):
+        base = START[level] - shift_rows
+
+        def init():
             return jnp.zeros((RANK, LANES), F32)
 
         def store(plane, value):
@@ -321,7 +331,7 @@
                         totals[p] = totals[p] + src_ref[pl.ds(at, 1), :] * tile_rows
                 return tuple(totals)
 
-            totals = lax.fori_loop(0, 3, slot, tuple(init(p) for p in range(block)))
+            totals = lax.fori_loop(0, 3, slot, tuple(init() for _ in range(block)))
             for p in range(block):
                 store(first + p, totals[p])
 
@@ -331,7 +341,7 @@
             lax.fori_loop(0, PLANES[level] // block, lambda b, c: (run(b * block), c)[1], 0)
 
 
-def top_kernel(par_ref, list_ref, g_ref, e_ref, s_ref, out_ref, m0_ref, m_ref, x_ref, t_ref, w_ref, src_ref, so_t, eo_t):
+def top_part(par_ref, list_ref, g_ref, e_ref, s_ref, out_ref, m0_ref, m_ref, x_ref, t_ref, w_ref, src_ref, so_t, eo_t):
     d = par_ref[0]
     identity = eye()
     for a in range(4):
@@ -398,15 +408,28 @@
         local = coupled
         for t in range(RANK):
             local = local + src_ref[t : t + 1, :] * eo_t[t * RANK : (t + 1) * RANK, :]
-    out_ref[...] = local
-
-
-def down_kernel(
-    par_ref, top_ref, c_ref, e_ref, four_ref, two_ref, ba_ref, near_ref, out_ref, l_ref, p_ref, z_ref, t_ref, w_ref
+    out_ref[0:RANK, :] = local
+
+
+def finish_kernel(
+    par_ref, list_ref, g_ref, te_ref, ts_ref, four_ref, two_ref, e_any, c0_any, c1_any, ba_any, n0, n1, n2, n3, out_any,
+    m0_ref, m_ref, x_ref, tb_ref, w_ref, src_ref, so_t, eo_t, l_ref, p_ref, z_ref, t_ref,
+    e_ref, c0_ref, c1_ref, ba_ref, near_ref, out_ref, sems,
 ):
+    copies = [
+        pltpu.make_async_copy(source, target, sems.at[j])
+        for j, (source, target) in enumerate(
+            [(e_any, e_ref), (c1_any, c1_ref), (c0_any, c0_ref), (ba_any, ba_ref)]
+            + [(n, near_ref.at[pl.ds(p * PART, PART)]) for p, n in enumerate((n0, n1, n2, n3))]
+        )
+    ]
+    for copy in copies:
+        copy.start()
+    top_part(par_ref, list_ref, g_ref, te_ref, ts_ref, l_ref, m0_ref, m_ref, x_ref, tb_ref, w_ref, src_ref, so_t, eo_t)
+    for copy in copies[:3]:
+        copy.wait()
     order = turn_order()
     transpose_swapped(order, tail_rows(e_ref, extra_rows(four_ref, two_ref, par_ref[0])), t_ref)
-    l_ref[0:RANK, :] = top_ref[...]
     for level in reversed(range(LEVELS)):
         if level > 0:
             spread_matrices(level, t_ref, w_ref)
@@ -427,7 +450,9 @@
             return w_ref[t * RANK : (t + 1) * RANK, :]
 
         def init(plane):
-            return c_ref[pl.ds(START[level] + plane * RANK, RANK), :]
+            if level == 0:
+                return c0_ref[plane_rows(plane), :]
+            return c1_ref[pl.ds(START[level] - START[1] + plane * RANK, RANK), :]
 
         def store(plane, value):
             l_ref[plane_rows(plane), :] = value
@@ -436,12 +461,23 @@
     for k in range(NK):
         z_ref[pl.ds(k, LANES, stride=NK), 0:RANK] = l_ref[k * RANK : (k + 1) * RANK, :].T
 
-    def leaf(i, carry):
-        local = z_ref[pl.ds(pl.multiple_of(i * NK, NK), NK), 0:RANK].astype(BF16)
-        out_ref[i] = near_ref[i] + dot(local, ba_ref[i])
-        return carry
-
-    lax.fori_loop(0, LANES, leaf, 0, unroll=8)
+    for copy in copies[3:]:
+        copy.wait()
+    sent = []
+    for part in range(PARTS):
+
+        def leaf(i, carry):
+            at = part * PART + i
+            local = z_ref[pl.ds(pl.multiple_of(at * NK, NK), NK), 0:RANK].astype(BF16)
+            out_ref[at] = near_ref[at] + dot(local, ba_ref[at])
+            return carry
+
+        lax.fori_loop(0, PART, leaf, 0, unroll=16)
+        rows = pl.ds(part * PART, PART)
+        sent.append(pltpu.make_async_copy(out_ref.at[rows], out_any.at[rows], sems.at[8 + part]))
+        sent[-1].start()
+    for copy in sent:
+        copy.wait()
 
 
 def three(x):
@@ -451,12 +487,26 @@
     return first, second, (rest - second).astype(BF16).astype(F32)
 
 
-def near_kernel(par_ref, list_ref, pt_ref, ch_ref, near_msg, far_msg, out_ref, fa_ref, fs_ref, fn_ref, k_ref):
+def near_kernel(part, *refs):
+    par_ref, list_ref, pt_ref, ch_ref, ptl_ref, chl_ref, ptr_ref, chr_ref = refs[:8]
+    out_ref, fa_ref, fs_ref, fn_ref, k_ref = refs[-5:]
     d = par_ref[0]
     odd = (d & 1) == 1
-    base = d * LANES
-    left = jnp.where(odd, near_msg[...], far_msg[...])
-    right = jnp.where(odd, far_msg[...], near_msg[...])
+    first_leaf = part * PART
+    base = d * LANES + first_leaf
+    left = [ptl_ref[c, 7:8, :] for c in range(3)]
+    right = [ptr_ref[c, 0:1, :] for c in range(3)]
+    left_charges, right_charges = chl_ref[0], chr_ref[0]
+    if len(refs) > 13:
+        near_msg, far_msg = refs[8:10]
+        if part == 0:
+            halo = jnp.where(odd, near_msg[...], far_msg[...])
+            left = [halo[c : c + 1, :] for c in range(3)]
+            left_charges = halo[8:24, :].astype(BF16)
+        else:
+            halo = jnp.where(odd, far_msg[...], near_msg[...])
+            right = [halo[c : c + 1, :] for c in range(3)]
+            right_charges = halo[8:24, :].astype(BF16)
     soft = jnp.float32(SOFTENING) * (SCALE * SCALE)
     row8 = iota((FRAME, LANES), 0) & 7
     fa_ref[...] = jnp.where(row8 == 4, 1.0, 0.0)
@@ -475,23 +525,24 @@
                 put(ref, j, value)
 
     def put_own(ref, j, value):
-        ref[pl.ds(8 + j, LANES, stride=8), :] = value
+        ref[pl.ds(8 + j, PART, stride=8), :] = value
 
     def put_left(ref, j, value):
         ref[j : j + 1, :] = value
 
     def put_right(ref, j, value):
-        at = (LANES + 1) * 8 + j
+        at = (PART + 1) * 8 + j
         ref[at : at + 1, :] = value
 
-    features([pt_ref[0], pt_ref[1], pt_ref[2]], iota((LANES, LANES), 0) + base, put_own)
+    features([pt_ref[0], pt_ref[1], pt_ref[2]], iota((PART, LANES), 0) + base, put_own)
     one_leaf = iota((1, LANES), 0) + base
-    features([left[c : c + 1, :] for c in range(3)], one_leaf - 1, put_left)
-    features([right[c : c + 1, :] for c in range(3)], one_leaf + LANES, put_right)
+    features(left, one_leaf - 1, put_left)
+    features(right, one_leaf + PART, put_right)
 
     def lists(i, offset):
         wanted = base + i + offset
-        hit = (list_ref[0, i] == wanted) | (list_ref[1, i] == wanted) | (list_ref[2, i] == wanted)
+        at = first_leaf + i
+        hit = (list_ref[0, at] == wanted) | (list_ref[1, at] == wanted) | (list_ref[2, at] == wanted)
         return jnp.where(hit, 1.0, 0.0).astype(F32)
 
     def pieces(ref, w):
@@ -508,14 +559,13 @@
     def kernel_of(source, target):
         return lax.rsqrt(dot_tn(source, target)).astype(BF16)
 
-    first = dot(left[8:24, :].astype(BF16), kernel_of(source_of(0), target_of(fn_ref, 1)))
+    first = dot(left_charges, kernel_of(source_of(0), target_of(fn_ref, 1)))
 
     def fill(i, carry):
         both = jnp.concatenate([target_of(fs_ref, i + 1), target_of(fn_ref, i + 2)], axis=1)
         k_ref[i] = kernel_of(source_of(i + 1), both)
         return carry
 
-    lax.fori_loop(0, LANES, fill, 0, unroll=16)
 
     def step(i, carry, own, after):
         spread = dot(own, k_ref[i])
@@ -527,12 +577,19 @@
         onward = step(i, carry, ch_ref[i], ch_ref[i + 1])
         return lists(i + 1, -1) * onward
 
-    carry = lax.fori_loop(0, LANES - 1, body, lists(0, -1) * first, unroll=16)
-    step(LANES - 1, carry, ch_ref[LANES - 1], right[8:24, :].astype(BF16))
+    carry = lists(0, -1) * first
+    for i in range(AHEAD):
+        fill(i, 0)
+    for i in range(PART - 1):
+        if i + AHEAD < PART:
+            fill(i + AHEAD, 0)
+        carry = body(i, carry)
+    step(PART - 1, carry, ch_ref[PART - 1], right_charges)
 
 
 VMEM = pl.BlockSpec(memory_space=pltpu.VMEM)
 SMEM = pl.BlockSpec(memory_space=pltpu.SMEM)
+ANY = pl.BlockSpec(memory_space=pl.ANY)
 
 
 def scratch(*shape, dtype=F32):
@@ -547,7 +604,7 @@
     return pl.BlockSpec(dims, lambda i, par: (0,) * len(dims))
 
 
-NEAR_SCRATCH = [scratch(FRAME, LANES)] * 3 + [scratch(LANES, LANES, 2 * LANES, dtype=BF16)]
+NEAR_SCRATCH = [scratch(FRAME, LANES)] * 3 + [scratch(PART, LANES, 2 * LANES, dtype=BF16)]
 FOUR = pl.BlockSpec((8, 1024), lambda i, par: (par[0] >> 1, 0))
 TWO = pl.BlockSpec((8, 1024), lambda i, par: (64 + (par[0] >> 2), 0))
 FOUR_C = pl.BlockSpec((3, 8, 1024), lambda i, par: (0, par[0] >> 1, 0))
@@ -555,10 +612,9 @@
 LEAF_SPEC = pl.BlockSpec((HEAD, LANES), lambda i, par: (0, 0))
 
 
-def call(kernel, name, in_specs, out_specs, out_shape, scratch_shapes):
+def call(kernel, in_specs, out_specs, out_shape, scratch_shapes):
     return pl.pallas_call(
         kernel,
-        name=name,
         grid_spec=pltpu.PrefetchScalarGridSpec(
             num_scalar_prefetch=1,
             grid=(1,),
@@ -568,6 +624,15 @@
         ),
         out_shape=out_shape,
     )
+
+
+def hop_partner(device, bit):
+    if bit == 0 or bit & 1:
+        return device ^ (1 << bit)
+    low = bit - 1
+    place = (device >> low) & 3
+    other = (place + 1) & 3 if place & 1 else (place - 1) & 3
+    return device + ((other - place) << low)
 
 
 def on_device(
@@ -586,55 +651,85 @@
     message = HEAD + ROWS[0]
     moments, msg_near, msg_far, device_moment = call(
         up_kernel,
-        "up",
         [whole(LANES, NK, LANES), whole(3, LANES, LANES), whole(LANES, RANK, LANES), whole(248, 1024), FOUR, TWO],
-        [whole(M_ROWS, LANES), whole(message, LANES), whole(message, LANES), whole(LANES, 512)],
-        [shape(M_ROWS, LANES), shape(message, LANES), shape(message, LANES), shape(LANES, 512)],
+        [whole(M_ROWS, LANES), whole(message, LANES), whole(message, LANES), whole(1, 512)],
+        [shape(M_ROWS, LANES), shape(message, LANES), shape(message, LANES), shape(1, 512)],
         [scratch(2048, LANES), scratch(512, LANES), scratch(1024, LANES, dtype=BF16), scratch(1024, LANES)],
     )(par, charges, points_t, basis, transfer, top_transfer, top_transfer)
 
     halo_near = lax.ppermute(msg_near, "cluster", mates)
     halo_far = lax.ppermute(msg_far, "cluster", others)
-    gathered = lax.all_to_all(device_moment, "cluster", 0, 0, tiled=True)
-
-    near = call(
-        near_kernel,
-        "near",
-        [SMEM, whole(3, LANES, LANES), whole(LANES, NK, LANES), LEAF_SPEC, LEAF_SPEC],
-        whole(LANES, NK, LANES),
-        shape(LANES, NK, LANES),
-        NEAR_SCRATCH,
-    )(par, near_list.T, points_t, charges, halo_near, halo_far)
-
-    coupled = call(
-        couple_kernel,
-        "couple",
-        [
-            whole(M_ROWS, LANES),
-            whole(message, LANES),
-            whole(message, LANES),
-            whole(3, 1, 248),
+    gathered = device_moment
+    for bit in range(7):
+        partner = lax.ppermute(gathered, "cluster", [(i, hop_partner(i, bit)) for i in range(devices)])
+        upper = ((d >> bit) & 1) == 1
+        gathered = jnp.concatenate(
+            [jnp.where(upper, partner, gathered), jnp.where(upper, gathered, partner)], axis=0
+        )
+
+    near_list_t = near_list.T
+    near = []
+    for part in range(PARTS):
+        lower, upper_leaf = max(PART * part - 1, 0), min(PART * (part + 1), LANES - 1)
+        specs = [
             SMEM,
-            whole(3, 248, 1024),
-            FOUR_C,
-            TWO_C,
-        ],
-        whole(M_ROWS, LANES),
-        shape(M_ROWS, LANES),
-        [scratch(1536, LANES), scratch(3072, LANES, dtype=BF16), scratch(3072, LANES), scratch(8, 2 * LANES)],
-    )(par, moments, halo_near, halo_far, jnp.transpose(loc_lists, (2, 0, 1)), top_l, coupling, top_c, top_c)
-
-    top_local = call(
-        top_kernel,
-        "top",
+            pl.BlockSpec((3, PART, LANES), lambda i, par, p=part: (0, p, 0)),
+            pl.BlockSpec((PART, NK, LANES), lambda i, par, p=part: (p, 0, 0)),
+            pl.BlockSpec((3, 8, LANES), lambda i, par, p=lower: (0, p // 8, 0)),
+            pl.BlockSpec((1, NK, LANES), lambda i, par, p=lower: (p, 0, 0)),
+            pl.BlockSpec((3, 8, LANES), lambda i, par, p=upper_leaf: (0, p // 8, 0)),
+            pl.BlockSpec((1, NK, LANES), lambda i, par, p=upper_leaf: (p, 0, 0)),
+        ]
+        operands = [near_list_t, points_t, charges, points_t, charges, points_t, charges]
+        if part in (0, PARTS - 1):
+            specs += [LEAF_SPEC, LEAF_SPEC]
+            operands += [halo_near, halo_far]
+        near.append(
+            call(
+                functools.partial(near_kernel, part),
+                specs,
+                whole(PART, NK, LANES),
+                shape(PART, NK, LANES),
+                NEAR_SCRATCH,
+            )(par, *operands)
+        )
+
+    coupled = []
+    fine_lists = jnp.transpose(loc_lists, (2, 0, 1))
+    for levels in ((0,), tuple(range(1, LEVELS))):
+        out_rows = sum(ROWS[level] for level in levels)
+        coupled.append(
+            call(
+                functools.partial(couple_kernel, levels),
+                [
+                    whole(M_ROWS, LANES),
+                    whole(message, LANES),
+                    whole(message, LANES),
+                    whole(3, 1, 248),
+                    SMEM,
+                    whole(3, 248, 1024),
+                    FOUR_C,
+                    TWO_C,
+                ],
+                whole(out_rows, LANES),
+                shape(out_rows, LANES),
+                [scratch(1536, LANES), scratch(3072, LANES, dtype=BF16), scratch(3072, LANES), scratch(8, 2 * LANES)],
+            )(par, moments, halo_near, halo_far, fine_lists, top_l, coupling, top_c, top_c)
+        )
+
+    return call(
+        finish_kernel,
         [
             SMEM,
             whole(LANES, 512),
             pl.BlockSpec((256, 1024), lambda i, par: (3, 0)),
             pl.BlockSpec((3, 256, 1024), lambda i, par: (0, 3, 0)),
-        ],
-        whole(RANK, LANES),
-        shape(RANK, LANES),
+            FOUR,
+            TWO,
+        ]
+        + [ANY] * (4 + PARTS),
+        ANY,
+        shape(LANES, NK, LANES),
         [
             scratch(512, LANES),
             scratch(START[6], LANES),
@@ -644,31 +739,19 @@
             scratch(96, LANES),
             scratch(3072, LANES),
             scratch(1024, LANES),
-        ],
-    )(par, top_l, gathered, top_transfer, top_c)
-
-    return call(
-        down_kernel,
-        "down",
-        [
-            whole(RANK, LANES),
-            whole(M_ROWS, LANES),
-            whole(248, 1024),
-            FOUR,
-            TWO,
-            whole(LANES, RANK, LANES),
-            whole(LANES, NK, LANES),
-        ],
-        whole(LANES, NK, LANES),
-        shape(LANES, NK, LANES),
-        [
             scratch(512, LANES),
             scratch(512, LANES),
             scratch(2048, LANES),
             scratch(1024, LANES),
-            scratch(1024, LANES),
+            scratch(248, 1024, dtype=BF16),
+            scratch(ROWS[0], LANES),
+            scratch(M_ROWS - ROWS[0], LANES),
+            scratch(LANES, RANK, LANES, dtype=BF16),
+            scratch(LANES, NK, LANES),
+            scratch(LANES, NK, LANES),
+            pltpu.SemaphoreType.DMA((8 + PARTS,)),
         ],
-    )(par, top_local, coupled, transfer, top_transfer, top_transfer, basis, near)
+    )(par, top_l, gathered, top_transfer, top_c, top_transfer, top_transfer, transfer, *coupled, basis, *near)
 
 
 def solution(mesh):
@@ -684,6 +767,4 @@
         P(),
         P(),
     )
-    return jax.shard_map(
-        on_device, mesh=mesh, in_specs=placed, out_specs=P("cluster", None, None), check_vma=False
-    )
+    return jax.shard_map(on_device, mesh=mesh, in_specs=placed, out_specs=P("cluster", None, None), check_vma=False)

time: 78.2 us -> 85.6 us (1.095)
  the two profiles are of different devices: /device:TPU:1 before, /device:TPU:32 now
where the time goes in v1:
time: 85.6 us; the launch traced here: 85.2 us
  Pallas kernels  48.4 us (57%)
  starting transfers between devices  20.1 us (23%)
  waiting for transfers between devices  14.1 us (16%)
  other arithmetic  1.51 us (2%)
    pallas_call x2, Pallas kernels, on_device(): call(functools.partial(couple_kernel, levels), [whole(M_ROWS, LANES), who...  14.6 us
    ppermute x7, waiting for transfers between devices, on_device(): lax.ppermute(gathered, 'cluster', [(i, hop_partner(i, bit)) for i in rang...  14.1 us
    pallas_call x4, Pallas kernels, on_device(): call(functools.partial(near_kernel, part), specs, whole(PART, NK, LANES),...  12.7 us
    pallas_call x1, Pallas kernels, on_device(): call(finish_kernel, [SMEM, whole(LANES, 512), pl.BlockSpec((256, 1024), l...  12.5 us
    ppermute x7, starting transfers between devices, on_device(): lax.ppermute(gathered, 'cluster', [(i, hop_partner(i, bit)) for i in rang...  11.2 us
    ppermute x1, starting transfers between devices, on_device(): halo_far = lax.ppermute(msg_far, 'cluster', others)  8.88 us
    pallas_call x1, Pallas kernels, on_device(): call(up_kernel, [whole(LANES, NK, LANES), whole(3, LANES, LANES), whole(L...  8.52 us
  transfers between devices with their start and end apart: 9, of which 6 were waited for; matrix products, arithmetic and copies ran while one was open for 1% of the time, Pallas kernels for 7%

profile of v1, /device:TPU:32, one launch (start us, length us, event | category | flops | bytes accessed | tf_op | source)
XLA Modules:
  0.0 85.2 jit_solution(13477571266217140005)
XLA Ops:
  0.0 8.5 %shard_map.100 = (f32[1056,128]{1,0:T(8,128)}, f32[536,128]{1,0:T(8,128)}, f32[536,128]{1,0:T(8,128)}, f32[1,512]{1,0:T(1,128)}) custom-call(s32[1]{0:T(128)} %bitcast.par_ref.refs_0_, bf16[128,16,128]{2,1,0:T(8,128)(2,1)} %refs_7_.7, f32[3,128,128]{2,1,0:T(8,128)} %bitcast.15, bf16[128,32,128]{2,1,0:T(8,128)(2,1)} %ba_any.1, bf16[248,1024]{1,0:T(8,128)(2,1)} %bitcast.30, ...), custom_call_target="tpu_custom_call" | custom-call | tf_op jit(solution)/shard_map/pallas_call | solution.py:652
  8.5 0.0 collective-permute-start
  8.5 1.4 %collective-permute-done = f32[1,512]{1,0:T(1,128)S(1)} collective-permute-done((f32[1,512]{1,0:T(1,128)}, f32[1,512]{1,0:T(1,128)S(1)}, u32[]{:S(2)}, u32[]{:S(2)}) %collective-permute-start) | collective-permute-done | bytes 2080 | tf_op jit(solution)/shard_map/ppermute | solution.py:664
  9.9 0.7 broadcast_select_fusion.9
  10.6 1.6 %collective-permute-start.1 = (f32[2,512]{1,0:T(2,128)S(1)}, f32[2,512]{1,0:T(2,128)S(1)}, u32[]{:S(2)}, u32[]{:S(2)}) collective-permute-start(f32[2,512]{1,0:T(2,128)S(1)} %pad_maximum_fusion.6), channel_id=1, source_target_pairs={{0,2},{1,3},{2,0},{3,1},{4,6},{5,7},{6,4},{7,5},{8,10},{9,11},{10,... | collective-permute-start | bytes 12296 | tf_op jit(solution)/shard_map/ppermute | solution.py:664
  12.2 2.1 %collective-permute-done.1 = f32[2,512]{1,0:T(2,128)S(1)} collective-permute-done((f32[2,512]{1,0:T(2,128)S(1)}, f32[2,512]{1,0:T(2,128)S(1)}, u32[]{:S(2)}, u32[]{:S(2)}) %collective-permute-start.1) | collective-permute-done | bytes 4128 | tf_op jit(solution)/shard_map/ppermute | solution.py:664
  14.3 2.8 %collective-permute-start.2 = (f32[4,512]{1,0:T(4,128)S(1)}, f32[4,512]{1,0:T(4,128)S(1)}, u32[]{:S(2)}, u32[]{:S(2)}) collective-permute-start(f32[4,512]{1,0:T(4,128)S(1)} %pad_maximum_fusion.5), channel_id=1, source_target_pairs={{0,6},{1,7},{2,4},{3,5},{4,2},{5,3},{6,0},{7,1},{8,14},{9,15},{10,... | collective-permute-start | bytes 24584 | tf_op jit(solution)/shard_map/ppermute | solution.py:664
  17.1 2.1 %collective-permute-done.2 = f32[4,512]{1,0:T(4,128)S(1)} collective-permute-done((f32[4,512]{1,0:T(4,128)S(1)}, f32[4,512]{1,0:T(4,128)S(1)}, u32[]{:S(2)}, u32[]{:S(2)}) %collective-permute-start.2) | collective-permute-done | bytes 8224 | tf_op jit(solution)/shard_map/ppermute | solution.py:664
  19.3 1.6 %collective-permute-start.3 = (f32[8,512]{1,0:T(8,128)S(1)}, f32[8,512]{1,0:T(8,128)S(1)}, u32[]{:S(2)}, u32[]{:S(2)}) collective-permute-start(f32[8,512]{1,0:T(8,128)S(1)} %pad_maximum_fusion.4), channel_id=1, source_target_pairs={{0,8},{1,9},{2,10},{3,11},{4,12},{5,13},{6,14},{7,15},{8,0},{9,1},... | collective-permute-start | bytes 49160 | tf_op jit(solution)/shard_map/ppermute | solution.py:664
  20.9 2.2 %collective-permute-done.3 = f32[8,512]{1,0:T(8,128)S(1)} collective-permute-done((f32[8,512]{1,0:T(8,128)S(1)}, f32[8,512]{1,0:T(8,128)S(1)}, u32[]{:S(2)}, u32[]{:S(2)}) %collective-permute-start.3) | collective-permute-done | bytes 16416 | tf_op jit(solution)/shard_map/ppermute | solution.py:664
  23.1 3.1 %collective-permute-start.4 = (f32[16,512]{1,0:T(8,128)S(1)}, f32[16,512]{1,0:T(8,128)S(1)}, u32[]{:S(2)}, u32[]{:S(2)}) collective-permute-start(f32[16,512]{1,0:T(8,128)S(1)} %pad_maximum_fusion.3), channel_id=1, source_target_pairs={{0,24},{1,25},{2,26},{3,27},{4,28},{5,29},{6,30},{7,31},{8,16},{9,... | collective-permute-start | bytes 98312 | tf_op jit(solution)/shard_map/ppermute | solution.py:664
  26.2 2.1 %collective-permute-done.4 = f32[16,512]{1,0:T(8,128)S(1)} collective-permute-done((f32[16,512]{1,0:T(8,128)S(1)}, f32[16,512]{1,0:T(8,128)S(1)}, u32[]{:S(2)}, u32[]{:S(2)}) %collective-permute-start.4) | collective-permute-done | bytes 32800 | tf_op jit(solution)/shard_map/ppermute | solution.py:664
  28.3 0.1 collective-permute-start.5
  28.4 4.2 %collective-permute-done.5 = f32[32,512]{1,0:T(8,128)S(1)} collective-permute-done((f32[32,512]{1,0:T(8,128)S(1)}, f32[32,512]{1,0:T(8,128)S(1)}, u32[]{:S(2)}, u32[]{:S(2)}) %collective-permute-start.5) | collective-permute-done | bytes 65568 | tf_op jit(solution)/shard_map/ppermute | solution.py:664
  32.7 2.0 %collective-permute-start.6 = (f32[64,512]{1,0:T(8,128)S(1)}, f32[64,512]{1,0:T(8,128)S(1)}, u32[]{:S(2)}, u32[]{:S(2)}) collective-permute-start(f32[64,512]{1,0:T(8,128)S(1)} %pad_maximum_fusion.1), channel_id=1, source_target_pairs={{0,96},{1,97},{2,98},{3,99},{4,100},{5,101},{6,102},{7,103},{8,104... | collective-permute-start | bytes 393224 | tf_op jit(solution)/shard_map/ppermute | solution.py:664
  34.7 0.0 collective-permute-start.7
  34.7 8.9 %collective-permute-start.8 = (f32[536,128]{1,0:T(8,128)}, f32[536,128]{1,0:T(8,128)S(1)}, u32[]{:S(2)}, u32[]{:S(2)}) collective-permute-start(f32[536,128]{1,0:T(8,128)} %get-tuple-element.12), channel_id=1, source_target_pairs={{1,2},{2,1},{3,4},{4,3},{5,6},{6,5},{7,8},{8,7},{9,10},{10,9},{11,... | collective-permute-start | bytes 823304 | tf_op jit(solution)/shard_map/ppermute | solution.py:661
  43.6 3.2 %shard_map.104.n1 = f32[32,16,128]{2,1,0:T(8,128)} custom-call(s32[1]{0:T(128)} %bitcast.par_ref.refs_0_, s32[3,128]{1,0:T(4,128)} %bitcast.35, f32[3,128,128]{2,1,0:T(8,128)} %bitcast.16, bf16[128,16,128]{2,1,0:T(8,128)(2,1)} %refs_7_.7, f32[3,128,128]{2,1,0:T(8,128)} %bitcast.17, bf16[128,16,128]{2,1,0:T(8,128)(2,1)} %refs_7_.7, f32[3,128,128]{2,1,0:T(8,128)} %bitcast.18, ...), custom_call_target="tpu_custom_call" | custom-call | tf_op jit(solution)/shard_map/pallas_call | solution.py:688
  46.8 3.2 %shard_map.105.n2 = f32[32,16,128]{2,1,0:T(8,128)} custom-call(s32[1]{0:T(128)} %bitcast.par_ref.refs_0_, s32[3,128]{1,0:T(4,128)} %bitcast.36, f32[3,128,128]{2,1,0:T(8,128)} %bitcast.19, bf16[128,16,128]{2,1,0:T(8,128)(2,1)} %refs_7_.7, f32[3,128,128]{2,1,0:T(8,128)} %bitcast.20, bf16[128,16,128]{2,1,0:T(8,128)(2,1)} %refs_7_.7, f32[3,128,128]{2,1,0:T(8,128)} %bitcast.21, ...), custom_call_target="tpu_custom_call" | custom-call | tf_op jit(solution)/shard_map/pallas_call | solution.py:688
  50.0 0.0 collective-permute-done.6
  50.0 0.7 pad_maximum_fusion.g_ref
  50.7 0.0 collective-permute-done.7.near_ref.refs_8_
  50.7 0.0 copy-start
  50.7 0.0 collective-permute-done.8.far_ref.refs_9_
  50.7 0.0 copy-start.1
  50.7 0.7 copy-done
  51.4 0.1 copy-done.1
  51.5 9.1 %shard_map.102.c1_any = f32[544,128]{1,0:T(8,128)} custom-call(s32[1]{0:T(128)} %bitcast.par_ref.refs_0_, f32[1056,128]{1,0:T(8,128)} %get-tuple-element.10.m_ref, f32[536,128]{1,0:T(8,128)} %copy-done, f32[536,128]{1,0:T(8,128)} %copy-done.1, s32[3,1,248]{2,1,0:T(1,128)} %bitcast.39, s32[3,1020]{1,0:T(4,128)} %bitcast.32, bf16[3,248,1024]{2,1,0:T(8,128)(2,1)} %bitcast.28, ...), custom_call_target="tpu_custom_call" | custom-call | tf_op jit(solution)/shard_map/pallas_call | solution.py:702
  60.7 5.5 %shard_map.101.c0_any = f32[512,128]{1,0:T(8,128)} custom-call(s32[1]{0:T(128)} %bitcast.par_ref.refs_0_, f32[1056,128]{1,0:T(8,128)} %get-tuple-element.10.m_ref, f32[536,128]{1,0:T(8,128)} %copy-done, f32[536,128]{1,0:T(8,128)} %copy-done.1, s32[3,1,248]{2,1,0:T(1,128)} %bitcast.40, s32[3,1020]{1,0:T(4,128)} %bitcast.33, bf16[3,248,1024]{2,1,0:T(8,128)(2,1)} %bitcast.29, ...), custom_call_target="tpu_custom_call" | custom-call | tf_op jit(solution)/shard_map/pallas_call | solution.py:702
  66.2 3.2 %shard_map.103.n0 = f32[32,16,128]{2,1,0:T(8,128)} custom-call(s32[1]{0:T(128)} %bitcast.par_ref.refs_0_, s32[3,128]{1,0:T(4,128)} %bitcast.37, f32[3,128,128]{2,1,0:T(8,128)} %bitcast.22, bf16[128,16,128]{2,1,0:T(8,128)(2,1)} %refs_7_.7, f32[3,128,128]{2,1,0:T(8,128)} %bitcast.23, bf16[128,16,128]{2,1,0:T(8,128)(2,1)} %refs_7_.7, f32[3,128,128]{2,1,0:T(8,128)} %bitcast.24, ...), custom_call_target="tpu_custom_call" | custom-call | tf_op jit(solution)/shard_map/pallas_call | solution.py:688
  69.3 3.2 %shard_map.106.n3 = f32[32,16,128]{2,1,0:T(8,128)} custom-call(s32[1]{0:T(128)} %bitcast.par_ref.refs_0_, s32[3,128]{1,0:T(4,128)} %bitcast.38, f32[3,128,128]{2,1,0:T(8,128)} %bitcast.25, bf16[128,16,128]{2,1,0:T(8,128)(2,1)} %refs_7_.7, f32[3,128,128]{2,1,0:T(8,128)} %bitcast.26, bf16[128,16,128]{2,1,0:T(8,128)(2,1)} %refs_7_.7, f32[3,128,128]{2,1,0:T(8,128)} %bitcast.27, ...), custom_call_target="tpu_custom_call" | custom-call | tf_op jit(solution)/shard_map/pallas_call | solution.py:688
  72.5 12.5 %shard_map.107 = f32[128,16,128]{2,1,0:T(8,128)} custom-call(s32[1]{0:T(128)} %bitcast.par_ref.refs_0_, s32[3,1020]{1,0:T(4,128)} %bitcast.34, f32[128,512]{1,0:T(8,128)} %pad_maximum_fusion.g_ref, bf16[1016,1024]{1,0:T(8,128)(2,1)} %two_ref.3, bf16[3,1020,1024]{2,1,0:T(8,128)(2,1)} %bitcast.14, bf16[1016,1024]{1,0:T(8,128)(2,1)} %two_ref.3, ...), custom_call_target="tpu_custom_call" | custom-call | tf_op jit(solution)/shard_map/pallas_call | solution.py:720
  (12 shorter events, 0.1 us)
Async XLA Ops:
  8.5 1.4 %collective-permute-start = (f32[1,512]{1,0:T(1,128)}, f32[1,512]{1,0:T(1,128)S(1)}, u32[]{:S(2)}, u32[]{:S(2)}) collective-permute-start(f32[1,512]{1,0:T(1,128)} %get-tuple-element.9), channel_id=1, source_target_pairs={{0,1},{1,0},{2,3},{3,2},{4,5},{5,4},{6,7},{7,6},{8,9},{9,8},{10,11... | collective-permute-start | bytes 6152 | tf_op jit(solution)/shard_map/ppermute | solution.py:664
  10.6 3.7 %collective-permute-start.1 = (f32[2,512]{1,0:T(2,128)S(1)}, f32[2,512]{1,0:T(2,128)S(1)}, u32[]{:S(2)}, u32[]{:S(2)}) collective-permute-start(f32[2,512]{1,0:T(2,128)S(1)} %pad_maximum_fusion.6), channel_id=1, source_target_pairs={{0,2},{1,3},{2,0},{3,1},{4,6},{5,7},{6,4},{7,5},{8,10},{9,11},{10,... | collective-permute-start | bytes 12296 | tf_op jit(solution)/shard_map/ppermute | solution.py:664
  14.3 4.9 %collective-permute-start.2 = (f32[4,512]{1,0:T(4,128)S(1)}, f32[4,512]{1,0:T(4,128)S(1)}, u32[]{:S(2)}, u32[]{:S(2)}) collective-permute-start(f32[4,512]{1,0:T(4,128)S(1)} %pad_maximum_fusion.5), channel_id=1, source_target_pairs={{0,6},{1,7},{2,4},{3,5},{4,2},{5,3},{6,0},{7,1},{8,14},{9,15},{10,... | collective-permute-start | bytes 24584 | tf_op jit(solution)/shard_map/ppermute | solution.py:664
  19.3 3.8 %collective-permute-start.3 = (f32[8,512]{1,0:T(8,128)S(1)}, f32[8,512]{1,0:T(8,128)S(1)}, u32[]{:S(2)}, u32[]{:S(2)}) collective-permute-start(f32[8,512]{1,0:T(8,128)S(1)} %pad_maximum_fusion.4), channel_id=1, source_target_pairs={{0,8},{1,9},{2,10},{3,11},{4,12},{5,13},{6,14},{7,15},{8,0},{9,1},... | collective-permute-start | bytes 49160 | tf_op jit(solution)/shard_map/ppermute | solution.py:664
  23.1 5.2 %collective-permute-start.4 = (f32[16,512]{1,0:T(8,128)S(1)}, f32[16,512]{1,0:T(8,128)S(1)}, u32[]{:S(2)}, u32[]{:S(2)}) collective-permute-start(f32[16,512]{1,0:T(8,128)S(1)} %pad_maximum_fusion.3), channel_id=1, source_target_pairs={{0,24},{1,25},{2,26},{3,27},{4,28},{5,29},{6,30},{7,31},{8,16},{9,... | collective-permute-start | bytes 98312 | tf_op jit(solution)/shard_map/ppermute | solution.py:664
  28.3 4.3 %collective-permute-start.5 = (f32[32,512]{1,0:T(8,128)S(1)}, f32[32,512]{1,0:T(8,128)S(1)}, u32[]{:S(2)}, u32[]{:S(2)}) collective-permute-start(f32[32,512]{1,0:T(8,128)S(1)} %pad_maximum_fusion.2), channel_id=1, source_target_pairs={{0,32},{1,33},{2,34},{3,35},{4,36},{5,37},{6,38},{7,39},{8,40},{9,... | collective-permute-start | bytes 196616 | tf_op jit(solution)/shard_map/ppermute | solution.py:664
  32.7 17.2 %collective-permute-start.6 = (f32[64,512]{1,0:T(8,128)S(1)}, f32[64,512]{1,0:T(8,128)S(1)}, u32[]{:S(2)}, u32[]{:S(2)}) collective-permute-start(f32[64,512]{1,0:T(8,128)S(1)} %pad_maximum_fusion.1), channel_id=1, source_target_pairs={{0,96},{1,97},{2,98},{3,99},{4,100},{5,101},{6,102},{7,103},{8,104... | collective-permute-start | bytes 393224 | tf_op jit(solution)/shard_map/ppermute | solution.py:664
  34.7 16.0 %collective-permute-start.7 = (f32[536,128]{1,0:T(8,128)}, f32[536,128]{1,0:T(8,128)S(1)}, u32[]{:S(2)}, u32[]{:S(2)}) collective-permute-start(f32[536,128]{1,0:T(8,128)} %get-tuple-element.11), channel_id=1, source_target_pairs={{0,1},{1,0},{2,3},{3,2},{4,5},{5,4},{6,7},{7,6},{8,9},{9,8},{10,11... | collective-permute-start | bytes 823304 | tf_op jit(solution)/shard_map/ppermute | solution.py:660
  34.7 16.0 %collective-permute-start.8 = (f32[536,128]{1,0:T(8,128)}, f32[536,128]{1,0:T(8,128)S(1)}, u32[]{:S(2)}, u32[]{:S(2)}) collective-permute-start(f32[536,128]{1,0:T(8,128)} %get-tuple-element.12), channel_id=1, source_target_pairs={{1,2},{2,1},{3,4},{4,3},{5,6},{6,5},{7,8},{8,7},{9,10},{10,9},{11,... | collective-permute-start | bytes 823304 | tf_op jit(solution)/shard_map/ppermute | solution.py:661
  50.7 0.7 copy-start
  50.7 0.8 copy-start.1
